TPU v7x, 128 devices: a whole 4x4x4 slice. The times are simulated.
128 devices in a mesh: req: 16 (over y_hi, x, core), head: 8 (over y_lo, z).
Axes of the slice: x: 4, y: 4 (y_hi: 2, y_lo: 2; y = y_hi * 2 + y_lo), z: 4, core: 2. Of those that a mesh axis runs over, the one named last changes fastest.
Arguments:
- hidden: bfloat16 [512, 16, 2048], P('req', None, 'head'), may hold values from -6 to 6
- w_zx: bfloat16 [2048, 2, 4096], P(None, None, 'head'), may hold values from -0.125 to 0.125
- w_bc: bfloat16 [2048, 256], replicated, may hold values from -0.125 to 0.125
- w_dt: bfloat16 [2048, 64], P(None, 'head'), may hold values from -0.125 to 0.125
- conv_x_w: float32 [5, 4096], P(None, 'head'), may hold values from -3 to 3
- conv_bc_w: float32 [5, 256], replicated, may hold values from -3 to 3
- dt_bias: float32 [64], P('head'), may hold values from -4 to 0.5
- a_log: float32 [64], P('head'), may hold values from 0 to 2.5
- d_skip: float32 [64], P('head'), may hold values from 0.5 to 1.5
- norm_gain: float32 [4096], P('head'), may hold values from 0.1 to 1.9
- w_out: bfloat16 [4096, 2048], P('head'), may hold values from -0.09375 to 0.09375
- ssm_state: float32 [512, 64, 64, 128], P('req', 'head'), may hold values from -3 to 3
- conv_x_state: float32 [512, 3, 4096], P('req', None, 'head'), may hold values from -6 to 6
- conv_bc_state: float32 [512, 3, 256], P('req'), may hold values from -6 to 6
- slot: int32 [512], replicated, may hold values from 0 to 511, as said below
- lengths: int32 [512], replicated, may hold values from 0 to 16
- accepted: int32 [512], replicated, may hold values from 0 to 16
Outputs:
- out: bfloat16 [512, 16, 2048], P('req', None, 'head')
- new_state: float32 [512, 64, 64, 128], P('req', 'head')
- new_conv_x: float32 [512, 3, 4096], P('req', None, 'head')
- new_conv_bc: float32 [512, 3, 256], P('req')
Inputs may be any that keep to these rules, and one draw needn't show every extreme that they name: slot is a permutation of the pool rows; the requests of each aligned block of 32 requests have exactly 2 pool rows in each aligned block of 32 pool rows.
All inputs are finite; a program needn't handle non-finite values.
Results may differ from a plain program's by a relative error of at most 0.0082.
Values may be sent and summed in bfloat16 or wider, within the bound.
No kernel may reach another device: no remote copies, remote signals or barrier semaphores. Data moves between devices by JAX's collectives and lax.ppermute only.
A program may use at most 128 MiB of HBM per device.

v0:
```python
import jax
import jax.numpy as jnp
from jax import lax
from jax.sharding import PartitionSpec as P

highest = lax.Precision.HIGHEST


def conv_step(previous, inputs, taps):
    window = jnp.concatenate([previous, inputs.astype(jnp.float32)], axis=1)
    tail = taps.shape[0] - 1
    steps = inputs.shape[1]
    total = taps[tail] + taps[0] * window[:, 0:steps]
    for tap in range(1, tail):
        total = total + taps[tap] * window[:, tap : tap + steps]
    return (jax.nn.silu(total).astype(jnp.bfloat16), window)


def keep_rows(window, counted, tail):
    picks = counted[:, None] + jnp.arange(tail, dtype=jnp.int32)[None, :]
    return jnp.take_along_axis(window, picks[:, :, None], axis=1)


def scan_block(x_conv, bc_conv, dt_in, states, counted, dt_bias, a_log, d_skip):
    heads = states.shape[1]
    nstate = states.shape[3]
    blocks, steps, chans = x_conv.shape
    headdim = chans // heads
    xh = x_conv.astype(jnp.float32).reshape(blocks, steps, heads, headdim)
    bmat = bc_conv[..., :nstate].astype(jnp.float32)
    cmat = bc_conv[..., nstate:].astype(jnp.float32)
    step_size = jax.nn.softplus(dt_in.astype(jnp.float32) + dt_bias)
    rate = step_size * -jnp.exp(a_log)
    cumul = jnp.cumsum(rate, axis=1)
    carried = jnp.exp(cumul)[..., None] * jnp.einsum(
        "bhpn,btn->bthp", states, cmat, precision=highest
    )
    inner = jnp.einsum("btn,bsn->bts", cmat, bmat, precision=highest)
    places = jnp.arange(steps, dtype=jnp.int32)
    lower = (places[:, None] >= places[None, :])[None, :, :, None]
    spread = cumul[:, :, None, :] - cumul[:, None, :, :]
    factor = jnp.where(lower, jnp.exp(jnp.where(lower, spread, 0.0)), 0.0)
    factor = factor * inner[..., None] * step_size[:, None, :, :]
    within = jnp.einsum("btsh,bshp->bthp", factor, xh, precision=highest)
    mixed = (
        (carried + within + d_skip[:, None] * xh).reshape(blocks, steps, chans).astype(jnp.bfloat16)
    )
    live = (places[None, :] < counted[:, None])[..., None]
    total = jnp.sum(jnp.where(live, rate, 0.0), axis=1)
    remain = jnp.where(live, total[:, None, :] - cumul, 0.0)
    scaled = jnp.where(live, jnp.exp(remain) * step_size, 0.0)
    updated = jnp.exp(total)[:, :, None, None] * states
    updated = updated + jnp.einsum("bsh,bshp,bsn->bhpn", scaled, xh, bmat, precision=highest)
    return (mixed, updated)


def advance(
    x_pre,
    bc_pre,
    dt_pre,
    conv_x_prev,
    conv_bc_prev,
    states,
    counted,
    conv_x_w,
    conv_bc_w,
    dt_bias,
    a_log,
    d_skip,
):
    tail = conv_x_prev.shape[1]
    x_conv, x_window = conv_step(conv_x_prev, x_pre, conv_x_w)
    bc_conv, bc_window = conv_step(conv_bc_prev, bc_pre, conv_bc_w)
    mixed, updated = scan_block(x_conv, bc_conv, dt_pre, states, counted, dt_bias, a_log, d_skip)
    return (mixed, updated, keep_rows(x_window, counted, tail), keep_rows(bc_window, counted, tail))


def per_device(
    hidden,
    w_zx,
    w_bc,
    w_dt,
    conv_x_w,
    conv_bc_w,
    dt_bias,
    a_log,
    d_skip,
    norm_gain,
    w_out,
    ssm_state,
    conv_x_state,
    conv_bc_state,
    slot,
    lengths,
    accepted,
):
    local_requests, steps, width_part = hidden.shape
    width = w_zx.shape[0]
    local_inner = w_zx.shape[2]
    bc_cols = w_bc.shape[1]
    stacked = jnp.concatenate([w_zx.reshape(width, 2 * local_inner), w_bc, w_dt], axis=1)
    piece = lax.all_gather(hidden, "head", axis=2, tiled=True)
    projected = jnp.dot(
        piece.reshape(-1, piece.shape[2]), stacked, preferred_element_type=jnp.float32
    )
    projected = projected.astype(jnp.bfloat16).reshape(local_requests, steps, -1)
    gate_in = projected[..., :local_inner]
    x_in = projected[..., local_inner : 2 * local_inner]
    bc_in = projected[..., 2 * local_inner : 2 * local_inner + bc_cols]
    dt_in = projected[..., 2 * local_inner + bc_cols :]
    myself = lax.axis_index("req")
    peers = lax.axis_size("req")
    per_peer = local_requests // peers
    slot_blocks = slot.reshape(peers, local_requests)
    owner_blocks = slot_blocks // local_requests
    local_rows = slot_blocks % local_requests
    by_owner = jnp.argsort(owner_blocks, axis=1, stable=True)
    my_order = lax.dynamic_index_in_dim(by_owner, myself, 0, keepdims=False)
    undo_order = jnp.argsort(my_order)
    selected = lax.dynamic_slice_in_dim(by_owner, myself * per_peer, per_peer, 1)
    arrive_rows = jnp.take_along_axis(local_rows, selected, axis=1).reshape(local_requests)
    to_pool = jnp.argsort(arrive_rows)
    counted = jnp.minimum(accepted, lengths)
    counted_blocks = counted.reshape(peers, local_requests)
    my_lengths = lax.dynamic_index_in_dim(
        lengths.reshape(peers, local_requests), myself, 0, keepdims=False
    )
    outgoing = (
        jnp.take(ssm_state, arrive_rows, axis=0),
        jnp.take(conv_x_state, arrive_rows, axis=0),
        jnp.take(conv_bc_state, arrive_rows, axis=0),
    )
    states_in, conv_x_in, conv_bc_in = (
        lax.all_to_all(outgoing[0], "req", split_axis=0, concat_axis=0, tiled=True),
        lax.all_to_all(outgoing[1], "req", split_axis=0, concat_axis=0, tiled=True),
        lax.all_to_all(outgoing[2], "req", split_axis=0, concat_axis=0, tiled=True),
    )
    my_counted = jnp.take(
        lax.dynamic_index_in_dim(counted_blocks, myself, 0, keepdims=False), my_order, axis=0
    )
    mixed_sorted, states_out, conv_x_out, conv_bc_out = advance(
        jnp.take(x_in, my_order, axis=0),
        jnp.take(bc_in, my_order, axis=0),
        jnp.take(dt_in, my_order, axis=0),
        conv_x_in,
        conv_bc_in,
        states_in,
        my_counted,
        conv_x_w,
        conv_bc_w,
        dt_bias,
        a_log,
        d_skip,
    )
    mixed = jnp.take(mixed_sorted, undo_order, axis=0)
    back_states, back_conv_x, back_conv_bc = (
        lax.all_to_all(states_out, "req", split_axis=0, concat_axis=0, tiled=True),
        lax.all_to_all(conv_x_out, "req", split_axis=0, concat_axis=0, tiled=True),
        lax.all_to_all(conv_bc_out, "req", split_axis=0, concat_axis=0, tiled=True),
    )
    new_state = jnp.take(back_states, to_pool, axis=0)
    new_conv_x = jnp.take(back_conv_x, to_pool, axis=0)
    new_conv_bc = jnp.take(back_conv_bc, to_pool, axis=0)
    gated = mixed.astype(jnp.float32) * jax.nn.silu(gate_in.astype(jnp.float32))
    squares = lax.psum(jnp.sum(gated * gated, axis=-1), "head")
    meansq = squares / (local_inner * lax.axis_size("head"))
    normed = (gated * lax.rsqrt(meansq + 1e-05)[..., None] * norm_gain).astype(jnp.bfloat16)
    partial_out = jnp.dot(
        normed.reshape(-1, local_inner), w_out, preferred_element_type=jnp.float32
    ).reshape(local_requests, steps, width)
    summed = lax.psum_scatter(partial_out, "head", scatter_dimension=2, tiled=True)
    places = jnp.arange(steps, dtype=jnp.int32)
    valid = places[None, :] < my_lengths[:, None]
    out = jnp.where(valid[..., None], summed, 0.0).astype(jnp.bfloat16)
    return (out, new_state, new_conv_x, new_conv_bc)


def solution(mesh):
    in_specs = (
        P("req", None, "head"),
        P(None, None, "head"),
        P(),
        P(None, "head"),
        P(None, "head"),
        P(),
        P("head"),
        P("head"),
        P("head"),
        P("head"),
        P("head", None),
        P("req", "head", None, None),
        P("req", None, "head"),
        P("req", None, None),
        P(),
        P(),
        P(),
    )
    out_specs = (
        P("req", None, "head"),
        P("req", "head", None, None),
        P("req", None, "head"),
        P("req", None, None),
    )
    return jax.shard_map(
        per_device, mesh=mesh, in_specs=in_specs, out_specs=out_specs, check_vma=False
    )
```

profile of v0, /device:TPU:1, one launch (start us, length us, event | category | flops | bytes accessed | tf_op | source)
XLA Modules:
  0.0 478.6 jit_solution(8611803134680669130)
XLA Ops:
  15.7 8.4 %all-to-all-start = ((f32[32,3,256]{2,1,0:T(4,128)}), f32[32,3,256]{2,1,0:T(4,128)S(1)}, u32[]{:S(2)}, u32[]{:S(2)}) async-start(f32[32,3,256]{2,1,0:T(4,128)} %copy_select_fusion), calls=%async_computation | async-start | bytes 262144 | tf_op jit(solution)/shard_map/all_to_all | solution.py:136
  25.9 7.9 %gather_fusion.7 = f32[32,8,64,128]{3,2,1,0:T(8,128)} fusion(f32[32,8,64,128]{3,2,1,0:T(8,128)} %param.36, s32[1024]{0:T(1024)S(1)} %pad_clamp_fusion.3), kind=kCustom, calls=%fused_computation.1.clone | custom fusion | bytes 16777344 | tf_op jit(solution)/shard_map/jit(_take)/gather | solution.py:129
  34.4 7.2 %all-to-all-start.2 = ((f32[32,3,512]{2,1,0:T(4,128)}), f32[32,3,512]{2,1,0:T(4,128)S(1)}, u32[]{:S(2)}, u32[]{:S(2)}) async-start(f32[32,3,512]{2,1,0:T(4,128)} %copy.86), calls=%async_computation.2 | async-start | bytes 524288 | tf_op jit(solution)/shard_map/all_to_all | solution.py:135
  41.6 8.8 %broadcast_select_fusion.1 = f32[32,8,64,128]{3,2,1,0:T(8,128)} fusion(f32[32,8,64,128]{3,2,1,0:T(8,128)} %gather_fusion.7, pred[32]{0:T(512)(128)(4,1)S(1)} %get-tuple-element.47), kind=kLoop, calls=%fused_computation.22 | loop fusion | flops 2097152 | bytes 16777248 | tf_op jit(solution)/shard_map/jit(_take)/select_n | solution.py:129
  51.2 7.2 %all-to-all-start.1 = ((f32[32,8,64,128]{3,2,1,0:T(8,128)}), f32[32,8,64,128]{3,2,1,0:T(8,128)}, u32[]{:S(2)}, u32[]{:S(2)}) async-start(f32[32,8,64,128]{3,2,1,0:T(8,128)} %broadcast_select_fusion.1), calls=%async_computation.1 | async-start | bytes 16777216 | tf_op jit(solution)/shard_map/all_to_all | solution.py:134
  59.7 5.4 %copy.101 = bf16[256,8,2,512]{3,1,2,0:T(8,128)(2,1)} copy(bf16[256,8,2,512]{3,2,1,0:T(2,128)(2,1)} %bitcast.56) | data formatting | bytes 8388608
  68.7 104.9 %all-gather.2.cloned.1.call-done = bf16[32,16,2048]{2,1,0:T(8,128)(2,1)} async-done(((bf16[32,16,256]{2,1,0:T(8,128)(2,1)}), bf16[32,16,2048]{2,1,0:T(8,128)(2,1)}) %all-gather.2.cloned.1.call-update) | async-done | bytes 2097168 | tf_op jit(solution)/shard_map/all_gather | solution.py:102
  173.6 7.6 %fusion.9 = bf16[512,1288]{0,1:T(8,128)(2,1)} fusion(bf16[512,2048]{1,0:T(8,128)(2,1)} %bitcast.68, bf16[2048,8]{1,0:T(8,128)(2,1)S(1)} %copy.77, bf16[2048,256]{1,0:T(8,128)(2,1)} %param.27, bf16[2048,1024]{1,0:T(8,128)(2,1)} %bitcast.57), kind=kOutput, calls=%fused_computation.28 | convolution fusion | flops 2717618176 | bytes 8691712 | tf_op jit(solution)/shard_map/dot_general | solution.py:103
  181.2 2.3 copy.78
  187.4 2.2 gather_fusion
  193.8 2.4 gather_fusion.1
  200.1 2.2 gather_fusion.5
  203.0 2.6 gather_fusion.9
  208.8 2.9 gather_fusion.4
  213.5 2.4 multiply_convert_fusion.1
  217.6 2.1 multiply_select_fusion
  226.9 2.4 multiply_convert_fusion.3
  231.3 2.9 fusion.16
  234.2 13.3 %all-to-all-start.5 = ((f32[32,3,256]{2,1,0:T(4,128)}), f32[32,3,256]{2,1,0:T(4,128)}, u32[]{:S(2)}, u32[]{:S(2)}) async-start(f32[32,3,256]{2,1,0:T(4,128)} %broadcast_select_fusion.6), calls=%async_computation.6 | async-start | bytes 262144 | tf_op jit(solution)/shard_map/all_to_all | solution.py:159
  247.6 13.9 %fusion.13 = bf16[32,16,8,64]{3,1,2,0:T(8,128)(2,1)S(1)} fusion(f32[32,8,64,16]{2,3,1,0:T(8,128)} %fusion.16, f32[32,8,64,128]{3,2,1,0:T(8,128)} %all-to-all-done.1, f32[8]{0:T(128)S(1)} %copy-done.25, f32[32,16,8]{1,2,0:T(8,128)} %copy.81, bf16[32,16,8,64]{3,2,1,0:T(8,128)(2,1)S(1)} %reshape.281, bf16[32,16,256]{2,1,0:T(8,128)(2,1)S(1)} %multiply_convert_fusion.3), kind=kOutput, calls=%fused_computation.32 | convolution fusion | flops 404226048 | bytes 11158016 | tf_op jit(solution)/shard_map/bhpn,btn->bthp/dot_general | solution.py:35
  262.7 2.6 convert_element_type.54
  265.3 2.6 gather_fusion.10
  267.8 13.1 %multiply_add_fusion = f32[32,8,64,128]{3,2,1,0:T(8,128)} fusion(f32[32,8,64,128]{3,2,1,0:T(8,128)} %all-to-all-done.1, f32[32,8]{1,0:T(8,128)S(1)} %copy-done.14, f32[32,16,8]{1,2,0:T(8,128)S(1)} %copy.93, bf16[32,16,8,64]{3,2,1,0:T(8,128)(2,1)S(1)} %reshape.281, bf16[32,16,256]{2,1,0:T(8,128)(2,1)S(1)} %multiply_convert_fusion.3), kind=kOutput, calls=%fused_computation.14 | convolution fusion | flops 407371776 | bytes 18104320 | tf_op jit(solution)/shard_map/bsh,bshp,bsn->bhpn/dot_general | solution.py:53
  282.5 26.1 %psum.7 = f32[32,16]{1,0:T(8,128)S(1)} all-reduce(f32[32,16]{1,0:T(8,128)S(1)} %multiply_reduce_fusion), channel_id=1, replica_groups=mesh['req'=16,'head'=8] {'head'}, use_global_device_ids=true, to_apply=%region_4.9 | all-reduce | flops 512 | bytes 4096 | tf_op jit(solution)/shard_map/psum | solution.py:165
  308.6 15.1 %all-to-all-start.4 = ((f32[32,3,512]{2,1,0:T(4,128)}), f32[32,3,512]{2,1,0:T(4,128)S(1)}, u32[]{:S(2)}, u32[]{:S(2)}) async-start(f32[32,3,512]{2,1,0:T(4,128)} %broadcast_select_fusion.3), calls=%async_computation.5 | async-start | bytes 524288 | tf_op jit(solution)/shard_map/all_to_all | solution.py:158
  323.7 8.6 %all-to-all-done.4 = f32[32,3,512]{2,1,0:T(4,128)S(1)} async-done(((f32[32,3,512]{2,1,0:T(4,128)}), f32[32,3,512]{2,1,0:T(4,128)S(1)}, u32[]{:S(2)}, u32[]{:S(2)}) %all-to-all-start.4) | async-done | bytes 196640 | tf_op jit(solution)/shard_map/all_to_all | solution.py:158
  332.4 5.3 %all-to-all-start.3 = ((f32[32,8,64,128]{3,2,1,0:T(8,128)}), f32[32,8,64,128]{3,2,1,0:T(8,128)}, u32[]{:S(2)}, u32[]{:S(2)}) async-start(f32[32,8,64,128]{3,2,1,0:T(8,128)} %multiply_add_fusion), calls=%async_computation.4 | async-start | bytes 16777216 | tf_op jit(solution)/shard_map/all_to_all | solution.py:157
  337.7 4.6 fusion.14
  348.6 103.6 %all-to-all-done.3 = f32[32,8,64,128]{3,2,1,0:T(8,128)} async-done(((f32[32,8,64,128]{3,2,1,0:T(8,128)}), f32[32,8,64,128]{3,2,1,0:T(8,128)}, u32[]{:S(2)}, u32[]{:S(2)}) %all-to-all-start.3) | async-done | bytes 8388640 | tf_op jit(solution)/shard_map/all_to_all | solution.py:157
  452.3 8.0 %gather_fusion.11 = f32[32,8,64,128]{3,2,1,0:T(8,128)} fusion(f32[32,8,64,128]{3,2,1,0:T(8,128)} %all-to-all-done.3, s32[1024]{0:T(1024)S(1)} %pad_clamp_fusion), kind=kCustom, calls=%fused_computation.5.clone | custom fusion | bytes 16777344 | tf_op jit(solution)/shard_map/jit(_take)/gather | solution.py:161
  460.2 8.9 %broadcast_select_fusion = f32[32,8,64,128]{3,2,1,0:T(8,128)} fusion(f32[32,8,64,128]{3,2,1,0:T(8,128)} %gather_fusion.11, pred[32]{0:T(512)(128)(4,1)S(1)} %compare_and_fusion), kind=kLoop, calls=%fused_computation.21 | loop fusion | flops 2097152 | bytes 16777248 | tf_op jit(solution)/shard_map/jit(_take)/select_n | solution.py:161
  469.7 1.9 select_convert_fusion.1
  (148 shorter events, 54.7 us)
Async XLA Ops:
  7.2 330.5 %copy-start = (bf16[512,2048]{1,0:T(8,128)(2,1)S(1)}, bf16[512,2048]{1,0:T(8,128)(2,1)}, u32[]{:S(2)}) copy-start(bf16[512,2048]{1,0:T(8,128)(2,1)} %param.35) | copy-start | bytes 6291460
  11.6 1.3 copy-start.17
  11.8 2.4 copy-start.2
  12.5 11.6 %copy-start.1 = (f32[32,3,512]{2,0,1:T(8,128)S(1)}, f32[32,3,512]{2,0,1:T(8,128)}, u32[]{:S(2)}) copy-start(f32[32,3,512]{2,0,1:T(8,128)} %param.37) | copy-start | bytes 589828
  12.9 1.3 copy-start.19
  15.7 18.1 %all-to-all-start = ((f32[32,3,256]{2,1,0:T(4,128)}), f32[32,3,256]{2,1,0:T(4,128)S(1)}, u32[]{:S(2)}, u32[]{:S(2)}) async-start(f32[32,3,256]{2,1,0:T(4,128)} %copy_select_fusion), calls=%async_computation | async-start | bytes 262144 | tf_op jit(solution)/shard_map/all_to_all | solution.py:136
  34.4 16.1 %all-to-all-start.2 = ((f32[32,3,512]{2,1,0:T(4,128)}), f32[32,3,512]{2,1,0:T(4,128)S(1)}, u32[]{:S(2)}, u32[]{:S(2)}) async-start(f32[32,3,512]{2,1,0:T(4,128)} %copy.86), calls=%async_computation.2 | async-start | bytes 524288 | tf_op jit(solution)/shard_map/all_to_all | solution.py:135
  50.5 8.9 %copy-start.15 = (bf16[2048,8]{0,1:T(8,128)(2,1)S(1)}, bf16[2048,8]{0,1:T(8,128)(2,1)}, u32[]{:S(2)}) copy-start(bf16[2048,8]{0,1:T(8,128)(2,1)} %param.28) | copy-start | bytes 98308
  51.2 183.0 %all-to-all-start.1 = ((f32[32,8,64,128]{3,2,1,0:T(8,128)}), f32[32,8,64,128]{3,2,1,0:T(8,128)}, u32[]{:S(2)}, u32[]{:S(2)}) async-start(f32[32,8,64,128]{3,2,1,0:T(8,128)} %broadcast_select_fusion.1), calls=%async_computation.1 | async-start | bytes 16777216 | tf_op jit(solution)/shard_map/all_to_all | solution.py:134
  58.4 115.2 %all-gather.2.cloned.1.call-start = ((), (), s32[]{:S(2)}) async-start(), calls=%async_computation.7 | async-start | bytes 2359296 | tf_op jit(solution)/shard_map/all_gather | solution.py:102
  59.7 7.2 %copy-start.27 = (f32[8]{0:T(128)S(1)}, f32[8]{0:T(128)}, u32[]{:S(2)}) copy-start(f32[8]{0:T(128)} %param.32) | copy-start | bytes 100
  59.7 7.8 %copy-start.21 = (f32[5,256]{1,0:T(8,128)S(1)}, f32[5,256]{1,0:T(8,128)}, u32[]{:S(2)}) copy-start(f32[5,256]{1,0:T(8,128)} %param.30) | copy-start | bytes 15364
  59.7 8.4 %copy-start.18 = (f32[5,512]{1,0:T(8,128)S(1)}, f32[5,512]{1,0:T(8,128)}, u32[]{:S(2)}) copy-start(f32[5,512]{1,0:T(8,128)} %param.29) | copy-start | bytes 30724
  183.4 15.6 %copy-start.3 = (bf16[512,1288]{1,0:T(8,128)(2,1)}, bf16[512,1288]{1,0:T(8,128)(2,1)S(1)}, u32[]{:S(2)}) copy-start(bf16[512,1288]{1,0:T(8,128)(2,1)S(1)} %copy.78) | copy-start | bytes 3956740
  197.2 0.8 copy-start.4
  200.1 6.7 %copy-start.6 = (f32[32,3,512]{2,1,0:T(4,128)S(1)}, f32[32,3,512]{2,1,0:T(4,128)}, u32[]{:S(2)}) copy-start(f32[32,3,512]{2,1,0:T(4,128)} %copy-done.5) | copy-start | bytes 589828
  211.8 5.8 %copy-start.7 = (bf16[32,16,8]{2,0,1:T(8,128)(2,1)S(1)}, bf16[32,16,8]{2,0,1:T(8,128)(2,1)}, u32[]{:S(2)}) copy-start(bf16[32,16,8]{2,0,1:T(8,128)(2,1)} %copy.80) | copy-start | bytes 24580
  219.7 11.6 %copy-start.24 = (pred[16,16]{1,0:T(8,128)(4,1)S(1)}, pred[16,16]{1,0:T(8,128)(4,1)}, u32[]{:S(2)}) copy-start(pred[16,16]{1,0:T(8,128)(4,1)} %iota_compare_fusion.2) | copy-start | bytes 772
  225.2 6.1 %copy-start.12 = (f32[32,16,8]{1,2,0:T(8,128)S(1)}, f32[32,16,8]{1,2,0:T(8,128)}, u32[]{:S(2)}) copy-start(f32[32,16,8]{1,2,0:T(8,128)} %copy.89) | copy-start | bytes 49156
  225.2 6.1 %copy-start.13 = (f32[32,16,8]{1,2,0:T(8,128)S(1)}, f32[32,16,8]{1,2,0:T(8,128)}, u32[]{:S(2)}) copy-start(f32[32,16,8]{1,2,0:T(8,128)} %copy.87) | copy-start | bytes 49156
  231.3 16.3 %copy-start.25 = (f32[8]{0:T(128)S(1)}, f32[8]{0:T(128)}, u32[]{:S(2)}) copy-start(f32[8]{0:T(128)} %param.33) | copy-start | bytes 100
  234.2 74.4 %all-to-all-start.5 = ((f32[32,3,256]{2,1,0:T(4,128)}), f32[32,3,256]{2,1,0:T(4,128)}, u32[]{:S(2)}, u32[]{:S(2)}) async-start(f32[32,3,256]{2,1,0:T(4,128)} %broadcast_select_fusion.6), calls=%async_computation.6 | async-start | bytes 262144 | tf_op jit(solution)/shard_map/all_to_all | solution.py:159
  261.4 6.4 %copy-start.14 = (f32[32,8]{1,0:T(8,128)S(1)}, f32[32,8]{1,0:T(8,128)}, u32[]{:S(2)}) copy-start(f32[32,8]{1,0:T(8,128)} %exp.49) | copy-start | bytes 3076
  267.8 13.1 %copy-start.8 = (bf16[32,16,512]{2,1,0:T(8,128)(2,1)S(1)}, bf16[32,16,512]{2,1,0:T(8,128)(2,1)}, u32[]{:S(2)}) copy-start(bf16[32,16,512]{2,1,0:T(8,128)(2,1)} %gather_fusion.10) | copy-start | bytes 1572868
  267.8 13.1 %copy-start.22 = (pred[32]{0:T(512)(128)(4,1)S(1)}, pred[32]{0:T(512)(128)(4,1)}, u32[]{:S(2)}) copy-start(pred[32]{0:T(512)(128)(4,1)} %get-tuple-element.46) | copy-start | bytes 100
  308.6 23.7 %all-to-all-start.4 = ((f32[32,3,512]{2,1,0:T(4,128)}), f32[32,3,512]{2,1,0:T(4,128)S(1)}, u32[]{:S(2)}, u32[]{:S(2)}) async-start(f32[32,3,512]{2,1,0:T(4,128)} %broadcast_select_fusion.3), calls=%async_computation.5 | async-start | bytes 524288 | tf_op jit(solution)/shard_map/all_to_all | solution.py:158
  323.7 14.0 %copy-start.9 = (bf16[32,16,512]{2,1,0:T(8,128)(2,1)S(1)}, bf16[32,16,512]{2,1,0:T(8,128)(2,1)}, u32[]{:S(2)}) copy-start(bf16[32,16,512]{2,1,0:T(8,128)(2,1)} %gather_fusion.10) | copy-start | bytes 1572868
  323.7 14.0 %copy-start.23 = (pred[32]{0:T(512)(128)(4,1)S(1)}, pred[32]{0:T(512)(128)(4,1)}, u32[]{:S(2)}) copy-start(pred[32]{0:T(512)(128)(4,1)} %get-tuple-element.46) | copy-start | bytes 100
  323.7 14.0 %copy-start.26 = (f32[512]{0:T(512)S(1)}, f32[512]{0:T(512)}, u32[]{:S(2)}) copy-start(f32[512]{0:T(512)} %param.34) | copy-start | bytes 6148
  332.4 119.9 %all-to-all-start.3 = ((f32[32,8,64,128]{3,2,1,0:T(8,128)}), f32[32,8,64,128]{3,2,1,0:T(8,128)}, u32[]{:S(2)}, u32[]{:S(2)}) async-start(f32[32,8,64,128]{3,2,1,0:T(8,128)} %multiply_add_fusion), calls=%async_computation.4 | async-start | bytes 16777216 | tf_op jit(solution)/shard_map/all_to_all | solution.py:157
  337.6 132.1 %reduce-scatter.2.cloned.1.call-start = ((), (), s32[]{:S(2)}) async-start(), calls=%async_computation.8 | async-start | bytes 4718592 | tf_op jit(solution)/shard_map/reduce_scatter | solution.py:171
  342.3 0.8 copy-start.20
  (4 other events, 2.7 us)
Sparse Core Ops, SparseCore 0:
  60.8 112.7 all-gather.1
  342.4 127.2 reduce-scatter.1
where the time goes:
time: 487 us; the launch traced here: 479 us
  waiting for transfers between devices  218 us (45%)
  local copies, waits for them, and re-layouts  75.2 us (15%)
  starting transfers between devices  56.6 us (12%)
  other arithmetic  45.3 us (9%)
  matrix products  42.2 us (9%)
  blocking collectives  26.1 us (5%)
  between operations  14.7 us (3%)
    all_gather x1, waiting for transfers between devices, per_device(): piece = lax.all_gather(hidden, 'head', axis=2, tiled=True)  105 us
    all_to_all x1, waiting for transfers between devices, per_device(): lax.all_to_all(states_out, 'req', split_axis=0, concat_axis=0, tiled=True)  104 us
    psum x1, blocking collectives, per_device(): squares = lax.psum(jnp.sum(gated * gated, axis=-1), 'head')  26.1 us
    all_to_all x1, starting transfers between devices, per_device(): lax.all_to_all(conv_x_out, 'req', split_axis=0, concat_axis=0, tiled=True)  15.1 us
    dot_general x1, matrix products, scan_block(): jnp.einsum('bhpn,btn->bthp', states, cmat, precision=highest)  13.9 us
    all_to_all x1, starting transfers between devices, per_device(): lax.all_to_all(conv_bc_out, 'req', split_axis=0, concat_axis=0, tiled=True)  13.3 us
    dot_general x1, matrix products, scan_block(): jnp.einsum('bsh,bshp,bsn->bhpn', scaled, xh, bmat, precision=highest)  13.1 us
    unnamed x61, local copies, waits for them, and re-layouts  12.2 us
  transfers between devices with their start and end apart: 8, of which 4 were waited for; matrix products, arithmetic and copies ran while one was open for 31% of the time, Pallas kernels for 0%

commit v1 on v0

--- a/solution.py
+++ b/solution.py
@@ -99,7 +99,9 @@
     local_inner = w_zx.shape[2]
     bc_cols = w_bc.shape[1]
     stacked = jnp.concatenate([w_zx.reshape(width, 2 * local_inner), w_bc, w_dt], axis=1)
-    piece = lax.all_gather(hidden, "head", axis=2, tiled=True)
+    piece = jnp.concatenate(
+        lax.all_to_all(jnp.stack([hidden] * lax.axis_size("head")), "head", 0, 0), axis=2
+    )
     projected = jnp.dot(
         piece.reshape(-1, piece.shape[2]), stacked, preferred_element_type=jnp.float32
     )

time: 487 us -> 438 us (0.90)
  waiting for transfers between devices: 218 us -> 172 us
  blocking collectives: 26.1 us -> 37.9 us
  starting transfers between devices: 56.6 us -> 46.4 us
    all_gather x1 -> x0, waiting for transfers between devices: 105 us -> none  [per_device(): piece = lax.all_gather(hidden, 'head', axis=2, tiled=True)]
    all_to_all x1, waiting for transfers between devices: 0.01 us -> 42.4 us  [per_device(): lax.all_to_all(outgoing[0], 'req', split_axis=0, concat_axis=0, tiled=True)]
    all_to_all x0 -> x1, blocking collectives: none -> 12.3 us  [per_device(): lax.all_to_all(outgoing[1], 'req', split_axis=0, concat_axis=0, tiled=True)]
    all_to_all x1, waiting for transfers between devices: 0.01 us -> 10 us  [per_device(): lax.all_to_all(jnp.stack([hidden] * lax.axis_size('head')), 'head', 0, 0)]
    all_to_all x1, waiting for transfers between devices: 0.01 us -> 6.5 us  [per_device(): lax.all_to_all(outgoing[2], 'req', split_axis=0, concat_axis=0, tiled=True)]
    all_to_all x1, starting transfers between devices: 13.3 us -> 7.05 us  [per_device(): lax.all_to_all(conv_bc_out, 'req', split_axis=0, concat_axis=0, tiled=True)]
    unnamed x61 -> x64, local copies, waits for them, and re-layouts: 12.2 us -> 10.1 us
  transfers between devices with their start and end apart: 8 -> 7, of which waited for: 4 -> 6; matrix products, arithmetic and copies ran while one was open for 31% -> 34% of each run, Pallas kernels for 0% -> 0%
where the time goes in v1:
time: 438 us; the launch traced here: 433 us
  waiting for transfers between devices  172 us (39%)
  local copies, waits for them, and re-layouts  77.3 us (18%)
  starting transfers between devices  46.4 us (11%)
  other arithmetic  45.4 us (10%)
  matrix products  39.1 us (9%)
  blocking collectives  37.9 us (9%)
  between operations  14.8 us (3%)
    all_to_all x1, waiting for transfers between devices, per_device(): lax.all_to_all(states_out, 'req', split_axis=0, concat_axis=0, tiled=True)  104 us
    all_to_all x1, waiting for transfers between devices, per_device(): lax.all_to_all(outgoing[0], 'req', split_axis=0, concat_axis=0, tiled=True)  42.4 us
    psum x1, blocking collectives, per_device(): squares = lax.psum(jnp.sum(gated * gated, axis=-1), 'head')  25.6 us
    all_to_all x1, starting transfers between devices, per_device(): lax.all_to_all(conv_x_out, 'req', split_axis=0, concat_axis=0, tiled=True)  14.9 us
    dot_general x1, matrix products, scan_block(): jnp.einsum('bhpn,btn->bthp', states, cmat, precision=highest)  13.9 us
    dot_general x1, matrix products, scan_block(): jnp.einsum('bsh,bshp,bsn->bhpn', scaled, xh, bmat, precision=highest)  13.1 us
    all_to_all x1, blocking collectives, per_device(): lax.all_to_all(outgoing[1], 'req', split_axis=0, concat_axis=0, tiled=True)  12.3 us
    unnamed x64, local copies, waits for them, and re-layouts  10.1 us
  transfers between devices with their start and end apart: 7, of which 6 were waited for; matrix products, arithmetic and copies ran while one was open for 34% of the time, Pallas kernels for 0%

profile of v1, /device:TPU:1, one launch (start us, length us, event | category | flops | bytes accessed | tf_op | source)
XLA Modules:
  0.0 432.6 jit_solution(7025657091842731608)
XLA Ops:
  15.7 8.4 %all-to-all-start.1 = ((f32[32,3,256]{2,1,0:T(4,128)}), f32[32,3,256]{2,1,0:T(4,128)S(1)}, u32[]{:S(2)}, u32[]{:S(2)}) async-start(f32[32,3,256]{2,1,0:T(4,128)} %copy_select_fusion), calls=%async_computation.1 | async-start | bytes 262144 | tf_op jit(solution)/shard_map/all_to_all | solution.py:138
  25.3 6.5 %all-to-all-done.1 = f32[32,3,256]{2,1,0:T(4,128)S(1)} async-done(((f32[32,3,256]{2,1,0:T(4,128)}), f32[32,3,256]{2,1,0:T(4,128)S(1)}, u32[]{:S(2)}, u32[]{:S(2)}) %all-to-all-start.1) | async-done | bytes 98336 | tf_op jit(solution)/shard_map/all_to_all | solution.py:138
  31.8 12.3 %all_to_all.35 = f32[32,3,512]{2,1,0:T(4,128)} all-to-all(f32[32,3,512]{2,1,0:T(4,128)S(1)} %copy.87), channel_id=1, replica_groups=mesh['req'=16,'head'=8] {'req'}, dimensions={0} | all-to-all | bytes 393216 | tf_op jit(solution)/shard_map/all_to_all | solution.py:137
  45.6 5.1 %all-to-all-start = ((bf16[8,32,16,256]{3,2,1,0:T(8,128)(2,1)}), bf16[8,32,16,256]{3,2,1,0:T(8,128)(2,1)}, u32[]{:S(2)}, u32[]{:S(2)}) async-start(bf16[8,32,16,256]{3,2,1,0:T(8,128)(2,1)} %stack.2), calls=%async_computation | async-start | bytes 4194304 | tf_op jit(solution)/shard_map/all_to_all | solution.py:103
  50.7 7.9 %gather_fusion.7 = f32[32,8,64,128]{3,2,1,0:T(8,128)} fusion(f32[32,8,64,128]{3,2,1,0:T(8,128)} %param.36, s32[1024]{0:T(1024)S(1)} %pad_clamp_fusion.3), kind=kCustom, calls=%fused_computation.1.clone | custom fusion | bytes 16777344 | tf_op jit(solution)/shard_map/jit(_take)/gather | solution.py:131
  58.6 8.8 %broadcast_select_fusion.1 = f32[32,8,64,128]{3,2,1,0:T(8,128)} fusion(f32[32,8,64,128]{3,2,1,0:T(8,128)} %gather_fusion.7, pred[32]{0:T(512)(128)(4,1)S(1)} %get-tuple-element.47), kind=kLoop, calls=%fused_computation.22 | loop fusion | flops 2097152 | bytes 16777248 | tf_op jit(solution)/shard_map/jit(_take)/select_n | solution.py:131
  67.5 10.0 %all-to-all-done = bf16[8,32,16,256]{3,2,1,0:T(8,128)(2,1)} async-done(((bf16[8,32,16,256]{3,2,1,0:T(8,128)(2,1)}), bf16[8,32,16,256]{3,2,1,0:T(8,128)(2,1)}, u32[]{:S(2)}, u32[]{:S(2)}) %all-to-all-start) | async-done | bytes 2097184 | tf_op jit(solution)/shard_map/all_to_all | solution.py:103
  77.5 5.5 %all-to-all-start.2 = ((f32[32,8,64,128]{3,2,1,0:T(8,128)}), f32[32,8,64,128]{3,2,1,0:T(8,128)}, u32[]{:S(2)}, u32[]{:S(2)}) async-start(f32[32,8,64,128]{3,2,1,0:T(8,128)} %broadcast_select_fusion.1), calls=%async_computation.2 | async-start | bytes 16777216 | tf_op jit(solution)/shard_map/all_to_all | solution.py:136
  83.5 3.4 copy.102
  90.6 3.3 copy.78
  95.1 4.5 %fusion.9 = bf16[512,1288]{0,1:T(8,128)(2,1)} fusion(bf16[512,2048]{1,0:T(8,128)(2,1)S(1)} %bitcast.62, bf16[2048,8]{1,0:T(8,128)(2,1)S(1)} %copy.77, bf16[2048,256]{1,0:T(8,128)(2,1)S(1)} %copy-done.26, bf16[2048,1024]{1,0:T(8,128)(2,1)S(1)} %bitcast.61), kind=kOutput, calls=%fused_computation.28 | convolution fusion | flops 2717618176 | bytes 8691712 | tf_op jit(solution)/shard_map/dot_general | solution.py:105
  99.6 2.3 copy.79
  112.3 2.4 gather_fusion.1
  121.4 2.6 gather_fusion.9
  127.3 3.0 gather_fusion.4
  132.1 2.3 multiply_convert_fusion.1
  145.4 2.5 multiply_convert_fusion.3
  149.9 2.9 fusion.16
  152.8 42.4 %all-to-all-done.2 = f32[32,8,64,128]{3,2,1,0:T(8,128)} async-done(((f32[32,8,64,128]{3,2,1,0:T(8,128)}), f32[32,8,64,128]{3,2,1,0:T(8,128)}, u32[]{:S(2)}, u32[]{:S(2)}) %all-to-all-start.2) | async-done | bytes 8388640 | tf_op jit(solution)/shard_map/all_to_all | solution.py:136
  195.2 7.1 %all-to-all-start.6 = ((f32[32,3,256]{2,1,0:T(4,128)}), f32[32,3,256]{2,1,0:T(4,128)}, u32[]{:S(2)}, u32[]{:S(2)}) async-start(f32[32,3,256]{2,1,0:T(4,128)} %broadcast_select_fusion.6), calls=%async_computation.7 | async-start | bytes 262144 | tf_op jit(solution)/shard_map/all_to_all | solution.py:161
  202.3 13.9 %fusion.13 = bf16[32,16,8,64]{3,1,2,0:T(8,128)(2,1)S(1)} fusion(f32[32,8,64,16]{2,3,1,0:T(8,128)} %fusion.16, f32[32,8,64,128]{3,2,1,0:T(8,128)} %all-to-all-done.2, f32[8]{0:T(128)S(1)} %copy-done.25, f32[32,16,8]{1,2,0:T(8,128)} %copy.82, bf16[32,16,8,64]{3,2,1,0:T(8,128)(2,1)S(1)} %reshape.283, bf16[32,16,256]{2,1,0:T(8,128)(2,1)S(1)} %multiply_convert_fusion.3), kind=kOutput, calls=%fused_computation.32 | convolution fusion | flops 404226048 | bytes 11158016 | tf_op jit(solution)/shard_map/bhpn,btn->bthp/dot_general | solution.py:35
  217.4 2.6 convert_element_type.54
  220.0 2.6 gather_fusion.10
  222.5 13.1 %multiply_add_fusion = f32[32,8,64,128]{3,2,1,0:T(8,128)} fusion(f32[32,8,64,128]{3,2,1,0:T(8,128)} %all-to-all-done.2, f32[32,8]{1,0:T(8,128)S(1)} %copy-done.14, f32[32,16,8]{1,2,0:T(8,128)S(1)} %copy.94, bf16[32,16,8,64]{3,2,1,0:T(8,128)(2,1)S(1)} %reshape.283, bf16[32,16,256]{2,1,0:T(8,128)(2,1)S(1)} %multiply_convert_fusion.3), kind=kOutput, calls=%fused_computation.14 | convolution fusion | flops 407371776 | bytes 18104320 | tf_op jit(solution)/shard_map/bsh,bshp,bsn->bhpn/dot_general | solution.py:53
  237.2 25.6 %psum.7 = f32[32,16]{1,0:T(8,128)S(1)} all-reduce(f32[32,16]{1,0:T(8,128)S(1)} %multiply_reduce_fusion), channel_id=1, replica_groups=mesh['req'=16,'head'=8] {'head'}, use_global_device_ids=true, to_apply=%region_4.9 | all-reduce | flops 512 | bytes 4096 | tf_op jit(solution)/shard_map/psum | solution.py:167
  262.7 14.9 %all-to-all-start.5 = ((f32[32,3,512]{2,1,0:T(4,128)}), f32[32,3,512]{2,1,0:T(4,128)S(1)}, u32[]{:S(2)}, u32[]{:S(2)}) async-start(f32[32,3,512]{2,1,0:T(4,128)} %broadcast_select_fusion.3), calls=%async_computation.6 | async-start | bytes 524288 | tf_op jit(solution)/shard_map/all_to_all | solution.py:160
  277.7 8.6 %all-to-all-done.5 = f32[32,3,512]{2,1,0:T(4,128)S(1)} async-done(((f32[32,3,512]{2,1,0:T(4,128)}), f32[32,3,512]{2,1,0:T(4,128)S(1)}, u32[]{:S(2)}, u32[]{:S(2)}) %all-to-all-start.5) | async-done | bytes 196640 | tf_op jit(solution)/shard_map/all_to_all | solution.py:160
  286.3 5.3 %all-to-all-start.4 = ((f32[32,8,64,128]{3,2,1,0:T(8,128)}), f32[32,8,64,128]{3,2,1,0:T(8,128)}, u32[]{:S(2)}, u32[]{:S(2)}) async-start(f32[32,8,64,128]{3,2,1,0:T(8,128)} %multiply_add_fusion), calls=%async_computation.5 | async-start | bytes 16777216 | tf_op jit(solution)/shard_map/all_to_all | solution.py:159
  291.7 4.5 %fusion.14 = f32[32,16,2048]{2,1,0:T(8,128)} fusion(bf16[512,2048]{1,0:T(8,128)(2,1)S(1)} %copy-done, f32[512]{0:T(512)S(1)} %copy-done.27, f32[32,16]{1,0:T(8,128)S(1)} %add_rsqrt_fusion, bf16[32,16,1288]{2,1,0:T(8,128)(2,1)} %bitcast.59, bf16[32,16,512]{2,1,0:T(8,128)(2,1)S(1)} %copy-done.8, pred[32]{0:T(512)(128)(4,1)S(1)} %copy-done.23), kind=kOutput, calls=%fused_computation.33 | convolution fusion | flops 1076625408 | bytes 7344160 | tf_op jit(solution)/shard_map/dot_general | solution.py:170
  302.6 103.6 %all-to-all-done.4 = f32[32,8,64,128]{3,2,1,0:T(8,128)} async-done(((f32[32,8,64,128]{3,2,1,0:T(8,128)}), f32[32,8,64,128]{3,2,1,0:T(8,128)}, u32[]{:S(2)}, u32[]{:S(2)}) %all-to-all-start.4) | async-done | bytes 8388640 | tf_op jit(solution)/shard_map/all_to_all | solution.py:159
  406.3 8.0 %gather_fusion.11 = f32[32,8,64,128]{3,2,1,0:T(8,128)} fusion(f32[32,8,64,128]{3,2,1,0:T(8,128)} %all-to-all-done.4, s32[1024]{0:T(1024)S(1)} %pad_clamp_fusion), kind=kCustom, calls=%fused_computation.5.clone | custom fusion | bytes 16777344 | tf_op jit(solution)/shard_map/jit(_take)/gather | solution.py:163
  414.2 8.9 %broadcast_select_fusion = f32[32,8,64,128]{3,2,1,0:T(8,128)} fusion(f32[32,8,64,128]{3,2,1,0:T(8,128)} %gather_fusion.11, pred[32]{0:T(512)(128)(4,1)S(1)} %compare_and_fusion), kind=kLoop, calls=%fused_computation.21 | loop fusion | flops 2097152 | bytes 16777248 | tf_op jit(solution)/shard_map/jit(_take)/select_n | solution.py:163
  (151 shorter events, 63.0 us)
Async XLA Ops:
  7.2 284.5 %copy-start = (bf16[512,2048]{1,0:T(8,128)(2,1)S(1)}, bf16[512,2048]{1,0:T(8,128)(2,1)}, u32[]{:S(2)}) copy-start(bf16[512,2048]{1,0:T(8,128)(2,1)} %param.35) | copy-start | bytes 6291460
  11.6 1.3 copy-start.17
  11.8 2.4 copy-start.2
  12.5 11.7 %copy-start.1 = (f32[32,3,512]{2,0,1:T(8,128)S(1)}, f32[32,3,512]{2,0,1:T(8,128)}, u32[]{:S(2)}) copy-start(f32[32,3,512]{2,0,1:T(8,128)} %param.37) | copy-start | bytes 589828
  12.9 1.3 copy-start.19
  14.9 29.1 %copy-start.10 = (bf16[32,16,256]{2,1,0:T(8,128)(2,1)S(1)}, bf16[32,16,256]{2,1,0:T(8,128)(2,1)}, u32[]{:S(2)}) copy-start(bf16[32,16,256]{2,1,0:T(8,128)(2,1)} %param.25) | copy-start | bytes 786436
  15.7 16.0 %all-to-all-start.1 = ((f32[32,3,256]{2,1,0:T(4,128)}), f32[32,3,256]{2,1,0:T(4,128)S(1)}, u32[]{:S(2)}, u32[]{:S(2)}) async-start(f32[32,3,256]{2,1,0:T(4,128)} %copy_select_fusion), calls=%async_computation.1 | async-start | bytes 262144 | tf_op jit(solution)/shard_map/all_to_all | solution.py:138
  31.8 13.8 %copy-start.9 = (f32[32,3,256]{2,1,0:T(4,128)}, f32[32,3,256]{2,1,0:T(4,128)S(1)}, u32[]{:S(2)}) copy-start(f32[32,3,256]{2,1,0:T(4,128)S(1)} %all-to-all-done.1) | copy-start | bytes 294916
  45.6 31.9 %all-to-all-start = ((bf16[8,32,16,256]{3,2,1,0:T(8,128)(2,1)}), bf16[8,32,16,256]{3,2,1,0:T(8,128)(2,1)}, u32[]{:S(2)}, u32[]{:S(2)}) async-start(bf16[8,32,16,256]{3,2,1,0:T(8,128)(2,1)} %stack.2), calls=%async_computation | async-start | bytes 4194304 | tf_op jit(solution)/shard_map/all_to_all | solution.py:103
  67.4 15.7 %copy-start.15 = (bf16[2048,8]{0,1:T(8,128)(2,1)S(1)}, bf16[2048,8]{0,1:T(8,128)(2,1)}, u32[]{:S(2)}) copy-start(bf16[2048,8]{0,1:T(8,128)(2,1)} %param.28) | copy-start | bytes 98308
  77.5 117.7 %all-to-all-start.2 = ((f32[32,8,64,128]{3,2,1,0:T(8,128)}), f32[32,8,64,128]{3,2,1,0:T(8,128)}, u32[]{:S(2)}, u32[]{:S(2)}) async-start(f32[32,8,64,128]{3,2,1,0:T(8,128)} %broadcast_select_fusion.1), calls=%async_computation.2 | async-start | bytes 16777216 | tf_op jit(solution)/shard_map/all_to_all | solution.py:136
  83.5 5.2 %copy-start.28 = (f32[8]{0:T(128)S(1)}, f32[8]{0:T(128)}, u32[]{:S(2)}) copy-start(f32[8]{0:T(128)} %param.32) | copy-start | bytes 100
  83.5 5.8 %copy-start.21 = (f32[5,256]{1,0:T(8,128)S(1)}, f32[5,256]{1,0:T(8,128)}, u32[]{:S(2)}) copy-start(f32[5,256]{1,0:T(8,128)} %param.30) | copy-start | bytes 15364
  83.5 6.4 %copy-start.18 = (f32[5,512]{1,0:T(8,128)S(1)}, f32[5,512]{1,0:T(8,128)}, u32[]{:S(2)}) copy-start(f32[5,512]{1,0:T(8,128)} %param.29) | copy-start | bytes 30724
  93.9 1.2 copy-start.26
  102.0 15.5 %copy-start.3 = (bf16[512,1288]{1,0:T(8,128)(2,1)}, bf16[512,1288]{1,0:T(8,128)(2,1)S(1)}, u32[]{:S(2)}) copy-start(bf16[512,1288]{1,0:T(8,128)(2,1)S(1)} %copy.79) | copy-start | bytes 3956740
  118.6 6.6 %copy-start.5 = (f32[32,3,512]{2,1,0:T(4,128)S(1)}, f32[32,3,512]{2,1,0:T(4,128)}, u32[]{:S(2)}) copy-start(f32[32,3,512]{2,1,0:T(4,128)} %all_to_all.35) | copy-start | bytes 589828
  130.3 5.8 %copy-start.6 = (bf16[32,16,8]{2,0,1:T(8,128)(2,1)S(1)}, bf16[32,16,8]{2,0,1:T(8,128)(2,1)}, u32[]{:S(2)}) copy-start(bf16[32,16,8]{2,0,1:T(8,128)(2,1)} %copy.81) | copy-start | bytes 24580
  138.2 11.7 %copy-start.24 = (pred[16,16]{1,0:T(8,128)(4,1)S(1)}, pred[16,16]{1,0:T(8,128)(4,1)}, u32[]{:S(2)}) copy-start(pred[16,16]{1,0:T(8,128)(4,1)} %iota_compare_fusion.2) | copy-start | bytes 772
  143.7 6.2 %copy-start.12 = (f32[32,16,8]{1,2,0:T(8,128)S(1)}, f32[32,16,8]{1,2,0:T(8,128)}, u32[]{:S(2)}) copy-start(f32[32,16,8]{1,2,0:T(8,128)} %copy.90) | copy-start | bytes 49156
  143.7 6.2 %copy-start.13 = (f32[32,16,8]{1,2,0:T(8,128)S(1)}, f32[32,16,8]{1,2,0:T(8,128)}, u32[]{:S(2)}) copy-start(f32[32,16,8]{1,2,0:T(8,128)} %copy.88) | copy-start | bytes 49156
  149.8 52.4 %copy-start.25 = (f32[8]{0:T(128)S(1)}, f32[8]{0:T(128)}, u32[]{:S(2)}) copy-start(f32[8]{0:T(128)} %param.33) | copy-start | bytes 100
  195.2 67.5 %all-to-all-start.6 = ((f32[32,3,256]{2,1,0:T(4,128)}), f32[32,3,256]{2,1,0:T(4,128)}, u32[]{:S(2)}, u32[]{:S(2)}) async-start(f32[32,3,256]{2,1,0:T(4,128)} %broadcast_select_fusion.6), calls=%async_computation.7 | async-start | bytes 262144 | tf_op jit(solution)/shard_map/all_to_all | solution.py:161
  216.1 6.4 %copy-start.14 = (f32[32,8]{1,0:T(8,128)S(1)}, f32[32,8]{1,0:T(8,128)}, u32[]{:S(2)}) copy-start(f32[32,8]{1,0:T(8,128)} %exp.49) | copy-start | bytes 3076
  222.5 13.1 %copy-start.7 = (bf16[32,16,512]{2,1,0:T(8,128)(2,1)S(1)}, bf16[32,16,512]{2,1,0:T(8,128)(2,1)}, u32[]{:S(2)}) copy-start(bf16[32,16,512]{2,1,0:T(8,128)(2,1)} %gather_fusion.10) | copy-start | bytes 1572868
  222.5 13.1 %copy-start.22 = (pred[32]{0:T(512)(128)(4,1)S(1)}, pred[32]{0:T(512)(128)(4,1)}, u32[]{:S(2)}) copy-start(pred[32]{0:T(512)(128)(4,1)} %get-tuple-element.46) | copy-start | bytes 100
  262.7 23.6 %all-to-all-start.5 = ((f32[32,3,512]{2,1,0:T(4,128)}), f32[32,3,512]{2,1,0:T(4,128)S(1)}, u32[]{:S(2)}, u32[]{:S(2)}) async-start(f32[32,3,512]{2,1,0:T(4,128)} %broadcast_select_fusion.3), calls=%async_computation.6 | async-start | bytes 524288 | tf_op jit(solution)/shard_map/all_to_all | solution.py:160
  277.7 14.0 %copy-start.8 = (bf16[32,16,512]{2,1,0:T(8,128)(2,1)S(1)}, bf16[32,16,512]{2,1,0:T(8,128)(2,1)}, u32[]{:S(2)}) copy-start(bf16[32,16,512]{2,1,0:T(8,128)(2,1)} %gather_fusion.10) | copy-start | bytes 1572868
  277.7 14.0 %copy-start.23 = (pred[32]{0:T(512)(128)(4,1)S(1)}, pred[32]{0:T(512)(128)(4,1)}, u32[]{:S(2)}) copy-start(pred[32]{0:T(512)(128)(4,1)} %get-tuple-element.46) | copy-start | bytes 100
  277.7 14.0 %copy-start.27 = (f32[512]{0:T(512)S(1)}, f32[512]{0:T(512)}, u32[]{:S(2)}) copy-start(f32[512]{0:T(512)} %param.34) | copy-start | bytes 6148
  286.3 119.9 %all-to-all-start.4 = ((f32[32,8,64,128]{3,2,1,0:T(8,128)}), f32[32,8,64,128]{3,2,1,0:T(8,128)}, u32[]{:S(2)}, u32[]{:S(2)}) async-start(f32[32,8,64,128]{3,2,1,0:T(8,128)} %multiply_add_fusion), calls=%async_computation.5 | async-start | bytes 16777216 | tf_op jit(solution)/shard_map/all_to_all | solution.py:159
  291.6 132.1 %reduce-scatter.2.cloned.1.call-start = ((), (), s32[]{:S(2)}) async-start(), calls=%async_computation.8 | async-start | bytes 4718592 | tf_op jit(solution)/shard_map/reduce_scatter | solution.py:173
  (4 other events, 2.8 us)
Sparse Core Ops, SparseCore 0:
  296.4 127.2 reduce-scatter.1
